TPU v7x, 32 devices: a whole 2x2x4 slice. The times are simulated.
32 devices in a mesh: head: 2 (over x), expert: 16 (over z, y, core).
Axes of the slice: x: 2, y: 2, z: 4, core: 2. Of those that a mesh axis runs over, the one named last changes fastest.
Arguments:
- queries: bfloat16 [256, 128, 576], P('expert', 'head'), may hold values from -64 to 64
- resident_cache: bfloat16 [64, 256, 576], P('expert'), may hold values from -6 to 6
- resident_len: int32 [64], P('expert'), may hold values from 1 to 256, as said below
- new_cache: bfloat16 [192, 64, 576], P('expert'), may hold values from -6 to 6
- new_len: int32 [192], replicated, may hold values from 1 to 64, as said below
- new_owner: int32 [192], replicated, may hold values from 0 to 15, as said below
- value_up: bfloat16 [128, 512, 128], P('head'), may hold values from -0.25 to 0.25
- w_output: bfloat16 [16384, 7168], P('head', 'expert'), may hold values from -0.046875 to 0.046875
- residual: bfloat16 [256, 7168], P(None, 'expert'), may hold values from -6 to 6
- expert_ids: int32 [256, 8], replicated, may hold values from 0 to 15, all different within a row; in each aligned block of 16 rows (0 to 15, 16 to 31, ...) at most 12 rows name the same one
- expert_gates: float32 [256, 8], replicated, may hold values from 0.1 to 1
- norm_gain: bfloat16 [7168], replicated, may hold values from 0.5 to 1.5
- w_gate: bfloat16 [16, 7168, 1024], P('expert', None, 'head'), may hold values from -0.0625 to 0.0625
- w_up: bfloat16 [16, 7168, 1024], P('expert', None, 'head'), may hold values from -0.0625 to 0.0625
- w_down: bfloat16 [16, 1024, 7168], P('expert', 'head'), may hold values from -0.1875 to 0.1875
Outputs:
- layer_out: bfloat16 [256, 7168], P('head', 'expert')
Inputs may be any that keep to these rules, and one draw needn't show every extreme that they name: `resident_len`: every decode owner has a resident request of length 256. `new_len`: every prefill device holds a new request of length 64. `new_owner`: one prefill device sends at most 2 of its 12 new requests to one decode owner, and every decode owner receives exactly 12 in all; a prefill device sends either 2 or none to each owner, except to at most one owner, which gets the remainder of 12 divided by 2. `expert_ids`: in each aligned block of 16 rows (the rows of one decode owner) no expert is named by more than 12 rows; the 8 experts of a row differ.
All inputs are finite; a program needn't handle non-finite values.
Results may differ from a plain program's by a relative error of at most 0.012.
Values may be sent and summed in bfloat16 or wider, within the bound.
A program may use at most 128 MiB of HBM per device.

v0:
```python
import jax
import jax.numpy as jnp
from jax import lax
from jax.sharding import PartitionSpec as P

ROPE = 64
NOPE = 128


def attend(queries, caches, length, value_up):
    inverse_root = (NOPE + ROPE) ** (-0.5)
    latent_width = value_up.shape[1]
    scores = (
        jnp.einsum("rhc,rtc->rht", queries, caches, preferred_element_type=jnp.float32)
        * inverse_root
    )
    inside = lax.broadcasted_iota(jnp.int32, scores.shape, 2) < length[:, None, None]
    scores = jnp.where(inside, scores, -jnp.inf)
    highest = jnp.max(scores, axis=2, keepdims=True)
    raised = jnp.exp(scores - highest)
    weights = (raised / jnp.sum(raised, axis=2, keepdims=True)).astype(jnp.bfloat16)
    latent = jnp.einsum(
        "rht,rtc->rhc", weights, caches[:, :, :latent_width], preferred_element_type=jnp.float32
    ).astype(jnp.bfloat16)
    values = jnp.einsum(
        "rhc,hcv->rhv", latent, value_up, preferred_element_type=jnp.float32
    ).astype(jnp.bfloat16)
    return values.reshape(values.shape[0], -1)


def earlier_equal(labels):
    count = labels.shape[0]
    position = jnp.arange(count, dtype=jnp.int32)
    before = (labels[:, None] == labels[None, :]) & (position[None, :] < position[:, None])
    return jnp.sum(before.astype(jnp.int32), axis=1)


def per_device(
    queries,
    resident_cache,
    resident_len,
    new_cache,
    new_len,
    new_owner,
    value_up,
    w_output,
    residual,
    expert_ids,
    expert_gates,
    norm_gain,
    w_gate,
    w_up,
    w_down,
):
    n_expert = lax.axis_size("expert")
    n_head = lax.axis_size("head")
    owner_index = lax.axis_index("expert")
    head_index = lax.axis_index("head")
    req_count = resident_cache.shape[0]
    new_count = new_cache.shape[0]
    rows_dev = req_count + new_count
    rows_all = rows_dev * n_expert
    choose = expert_ids.shape[1]
    local_experts = w_gate.shape[0]
    experts = local_experts * n_expert
    column_slab = residual.shape[1]
    most = max(2, (4 * new_count + 3 * n_expert - 1) // (3 * n_expert))
    capacity = max(2, 3 * rows_dev * choose // (2 * experts))
    slots_all = n_expert * capacity
    group = n_expert // n_head
    block_rows = group * rows_dev
    cache_shape = new_cache.shape[1:]
    targets = lax.dynamic_slice_in_dim(new_owner, owner_index * new_count, new_count)
    places = targets * most + earlier_equal(targets)
    senders = (
        jnp.full((n_expert * most,), new_count, jnp.int32)
        .at[places]
        .set(jnp.arange(new_count, dtype=jnp.int32))
    )
    outgoing = jnp.take(new_cache, senders, axis=0, mode="fill", fill_value=0).reshape(
        (n_expert, most) + cache_shape
    )
    incoming = lax.all_to_all(outgoing, "expert", split_axis=0, concat_axis=0, tiled=True)
    ordering = jnp.argsort(new_owner, stable=True)
    chosen = lax.dynamic_slice_in_dim(ordering, owner_index * new_count, new_count)
    anchor = chosen // new_count
    arrived = jnp.take(
        incoming.reshape((n_expert * most,) + cache_shape),
        anchor * most + earlier_equal(anchor),
        axis=0,
    )
    resident_att = attend(queries[:req_count], resident_cache, resident_len, value_up)
    arrived_att = attend(queries[req_count:], arrived, new_len[chosen], value_up)
    attention = jnp.concatenate([resident_att, arrived_att], axis=0)
    mixed = jnp.dot(
        lax.all_gather(attention, "expert", axis=0, tiled=True),
        w_output,
        preferred_element_type=jnp.float32,
    )
    picks = expert_ids.reshape(n_expert, rows_dev * choose)
    onehot = (picks[:, :, None] == jnp.arange(experts, dtype=jnp.int32)[None, None, :]).astype(
        jnp.int32
    )
    ranking = jnp.sum(jnp.cumsum(onehot, axis=1) * onehot, axis=2) - 1
    source = jnp.broadcast_to(jnp.arange(n_expert, dtype=jnp.int32)[:, None], picks.shape)
    slot_index = picks * slots_all + source * capacity + ranking
    row_index = (
        source * rows_dev + jnp.arange(rows_dev * choose, dtype=jnp.int32)[None, :] // choose
    )
    slot_rows = (
        jnp.full((experts * slots_all,), rows_all, jnp.int32)
        .at[slot_index.reshape(-1)]
        .set(row_index.reshape(-1))
    )
    summed = lax.psum(mixed, "head")
    hidden_all = (residual.astype(jnp.float32) + summed).astype(jnp.bfloat16)
    hidden_block = lax.dynamic_slice_in_dim(hidden_all, head_index * block_rows, block_rows)
    gathered = jnp.take(hidden_all, slot_rows, axis=0, mode="fill", fill_value=0).reshape(
        n_expert, local_experts * slots_all, column_slab
    )
    arrived_rows = lax.all_to_all(gathered, "expert", split_axis=0, concat_axis=2, tiled=True)
    inputs = arrived_rows.astype(jnp.float32)
    inverse = lax.rsqrt(jnp.mean(inputs * inputs, axis=2, keepdims=True) + 1e-06)
    normed = (inputs * inverse * norm_gain.astype(jnp.float32)).astype(jnp.bfloat16)
    gate_act = jnp.einsum("esd,edf->esf", normed, w_gate, preferred_element_type=jnp.float32)
    up_act = jnp.einsum("esd,edf->esf", normed, w_up, preferred_element_type=jnp.float32)
    hidden_act = (jax.nn.silu(gate_act) * up_act).astype(jnp.bfloat16)
    partial_value = jnp.einsum(
        "esf,efd->esd", hidden_act, w_down, preferred_element_type=jnp.float32
    )
    shared = lax.psum_scatter(
        partial_value.astype(jnp.bfloat16), "head", scatter_dimension=1, tiled=True
    ).astype(jnp.float32)
    returned = lax.all_to_all(
        shared.astype(jnp.bfloat16), "expert", split_axis=2, concat_axis=0, tiled=True
    ).astype(shared.dtype)
    ids_block = lax.dynamic_slice_in_dim(expert_ids, head_index * block_rows, block_rows)
    gates_block = lax.dynamic_slice_in_dim(expert_gates, head_index * block_rows, block_rows)
    source_block = (
        lax.dynamic_slice_in_dim(
            source.reshape(rows_all, choose), head_index * block_rows, block_rows
        )
        - head_index * group
    )
    rank_block = lax.dynamic_slice_in_dim(
        ranking.reshape(rows_all, choose), head_index * block_rows, block_rows
    )
    local_slot = ids_block * (group * capacity) + source_block * capacity + rank_block
    picked = jnp.take(
        returned.reshape(experts * group * capacity, column_slab), local_slot.reshape(-1), axis=0
    ).reshape(block_rows, choose, column_slab)
    routed_block = jnp.sum(picked * gates_block[:, :, None], axis=1)
    return (hidden_block.astype(jnp.float32) + routed_block).astype(jnp.bfloat16)


def solution(mesh):
    return jax.shard_map(
        per_device,
        mesh=mesh,
        in_specs=(
            P("expert", "head", None),
            P("expert", None, None),
            P("expert"),
            P("expert", None, None),
            P(),
            P(),
            P("head", None, None),
            P("head", "expert"),
            P(None, "expert"),
            P(),
            P(),
            P(),
            P("expert", None, "head"),
            P("expert", None, "head"),
            P("expert", "head", None),
        ),
        out_specs=P("head", "expert"),
        check_vma=False,
    )
```

profile of v0, /device:TPU:13, one launch (start us, length us, event | category | flops | bytes accessed | tf_op | source)
XLA Modules:
  0.0 468.8 jit_solution(2501718633419591748)
XLA Ops:
  7.6 3.8 sort.17
  15.3 3.5 broadcast_select_fusion.1
  18.9 6.7 %all-to-all-start = ((bf16[16,2,64,576]{3,2,1,0:T(8,128)(2,1)}), bf16[16,2,64,576]{3,2,1,0:T(8,128)(2,1)}, u32[]{:S(2)}, u32[]{:S(2)}) async-start(bf16[16,2,64,576]{3,2,1,0:T(8,128)(2,1)} %broadcast_select_fusion.1), calls=%async_computation | async-start | bytes 5242880 | tf_op jit(solution)/shard_map/all_to_all | solution.py:83
  30.1 4.6 fusion.28
  34.7 49.6 %all-to-all-done = bf16[16,2,64,576]{3,2,1,0:T(8,128)(2,1)} async-done(((bf16[16,2,64,576]{3,2,1,0:T(8,128)(2,1)}), bf16[16,2,64,576]{3,2,1,0:T(8,128)(2,1)}, u32[]{:S(2)}, u32[]{:S(2)}) %all-to-all-start) | async-done | bytes 2359328 | tf_op jit(solution)/shard_map/all_to_all | solution.py:83
  84.3 2.5 gather_fusion.2
  89.8 4.8 %fusion.26 = bf16[12,64,128]{2,0,1:T(8,128)(2,1)S(1)} fusion(bf16[64,512,128]{2,1,0:T(8,128)(2,1)} %param.21, bf16[12,64,512]{2,1,0:T(8,128)(2,1)S(1)} %convolution_convert_fusion.1), kind=kOutput, calls=%fused_computation.39 | convolution fusion | flops 100761600 | bytes 9371648 | tf_op jit(solution)/shard_map/rhc,hcv->rhv/dot_general | solution.py:25
  96.3 2.8 select_reduce_fusion
  99.6 45.6 %all-gather.2.cloned.1.call-done = bf16[256,8192]{1,0:T(8,128)(2,1)} async-done(((bf16[16,8192]{1,0:T(8,128)(2,1)}), bf16[256,8192]{1,0:T(8,128)(2,1)}) %all-gather.2.cloned.1.call-update) | async-done | bytes 4194320 | tf_op jit(solution)/shard_map/all_gather | solution.py:96
  145.2 7.2 %fusion.59 = f32[256,448]{0,1:T(8,128)} fusion(bf16[256,8192]{1,0:T(8,128)(2,1)} %all-gather.2.cloned.1.call-done, bf16[8192,448]{0,1:T(8,128)(2,1)} %param.22), kind=kOutput, calls=%fused_computation.117 | convolution fusion | flops 1879048192 | bytes 11993088 | tf_op jit(solution)/shard_map/dot_general | solution.py:95
  152.5 8.1 %scatter_custom_fusion.1 = s32[3072]{0:T(1024)S(1)} fusion(s32[2048]{0:T(1024)S(1)} %bitcast.83, s32[2048]{0:T(1024)S(1)} %add_bitcast_fusion, s32[]{:T(128)} %constant.124.clone.1), kind=kCustom, calls=%fused_computation.82 | custom fusion | bytes 12292 | tf_op jit(solution)/shard_map/scatter | solution.py:113
  160.7 18.0 %all-reduce.2.cloned.1.call-done = f32[256,448]{0,1:T(8,128)} async-done(((f32[256,448]{0,1:T(8,128)}), f32[256,448]{0,1:T(8,128)}) %all-reduce.2.cloned.1.call-update) | async-done | bytes 458768 | tf_op jit(solution)/shard_map/psum | solution.py:115
  179.9 13.2 %gather_fusion.3 = bf16[3072,448]{1,0:T(8,128)(2,1)} fusion(bf16[256,448]{1,0:T(8,128)(2,1)S(1)} %copy.104, s32[3072]{0:T(1024)S(1)} %fusion.47), kind=kCustom, calls=%fused_computation.3 | custom fusion | bytes 5517312 | tf_op jit(solution)/shard_map/jit(_take)/gather | solution.py:118
  193.1 3.4 broadcast_select_fusion
  196.5 6.6 %all-to-all-start.1 = ((bf16[16,192,448]{2,1,0:T(8,128)(2,1)}), bf16[16,192,448]{2,1,0:T(8,128)(2,1)}, u32[]{:S(2)}, u32[]{:S(2)}) async-start(bf16[16,192,448]{2,1,0:T(8,128)(2,1)} %broadcast_select_fusion), calls=%async_computation.1 | async-start | bytes 6291456 | tf_op jit(solution)/shard_map/all_to_all | solution.py:121
  203.2 69.9 %all-to-all-done.1 = bf16[16,192,448]{2,1,0:T(8,128)(2,1)} async-done(((bf16[16,192,448]{2,1,0:T(8,128)(2,1)}), bf16[16,192,448]{2,1,0:T(8,128)(2,1)}, u32[]{:S(2)}, u32[]{:S(2)}) %all-to-all-start.1) | async-done | bytes 2752544 | tf_op jit(solution)/shard_map/all_to_all | solution.py:121
  273.1 2.7 fusion.8
  275.8 2.8 fusion.11
  278.5 3.4 copy.105
  282.0 6.4 %convert_element_type.122 = bf16[192,7168]{1,0:T(8,128)(2,1)} reshape(bf16[1,192,16,448]{3,2,1,0:T(8,128)(2,1)} %copy.105) | data formatting | bytes 5505024 | tf_op jit(solution)/shard_map/convert_element_type | solution.py:124
  288.3 5.5 %fusion.6 = f32[192,512]{1,0:T(8,128)S(1)} fusion(bf16[192,7168]{1,0:T(8,128)(2,1)} %convert_element_type.122, bf16[1,7168,512]{2,1,0:T(8,128)(2,1)} %param.27), kind=kOutput, calls=%fused_computation.16 | convolution fusion | flops 1409286144 | bytes 10485760 | tf_op jit(solution)/shard_map/esd,edf->esf/dot_general | solution.py:125
  293.9 10.7 %fusion.2 = bf16[1,192,7168]{2,1,0:T(8,128)(2,1)} fusion(bf16[1,512,7168]{2,1,0:T(8,128)(2,1)} %param.29, bf16[192,7168]{1,0:T(8,128)(2,1)} %convert_element_type.122, bf16[1,7168,512]{2,1,0:T(8,128)(2,1)} %param.28, f32[192,512]{1,0:T(8,128)S(1)} %fusion.6), kind=kOutput, calls=%fused_computation.10 | convolution fusion | flops 2820538368 | bytes 20578304 | tf_op jit(solution)/shard_map/esf,efd->esd/dot_general | solution.py:128
  304.5 37.6 %reduce-scatter.2.cloned.1.call-done = bf16[1,96,7168]{2,1,0:T(8,128)(2,1)} async-done(((bf16[1,192,7168]{2,1,0:T(8,128)(2,1)}), bf16[1,96,7168]{2,1,0:T(8,128)(2,1)}) %reduce-scatter.2.cloned.1.call-update) | async-done | bytes 1376272 | tf_op jit(solution)/shard_map/reduce_scatter | solution.py:131
  342.1 8.5 %copy.106 = bf16[1,96,7168]{1,0,2:T(2,128)(2,1)} copy(bf16[1,96,7168]{2,1,0:T(8,128)(2,1)} %reduce-scatter.2.cloned.1.call-done) | data formatting | bytes 2752512 | tf_op jit(solution)/shard_map/reduce_scatter | solution.py:131
  351.1 39.8 %reduce.3 = bf16[7168,96]{1,0:T(8,128)(2,1)S(1)} reduce(bf16[7168,1,96]{2,1,0:T(2,128)(2,1)} %bitcast.74, bf16[]{:T(256)} %broadcast.267), dimensions={1}, to_apply=%bitcast.57.reduce_sub_computation | reduce | bytes 2752514
  390.9 3.9 reshape.370
  394.8 6.5 %all-to-all-start.2 = ((bf16[16,2,21504]{2,1,0:T(2,128)(2,1)}), bf16[16,2,21504]{2,1,0:T(2,128)(2,1)S(1)}, u32[]{:S(2)}, u32[]{:S(2)}) async-start(bf16[16,2,21504]{2,1,0:T(2,128)(2,1)} %reshape.370), calls=%async_computation.3 | async-start | bytes 2752512 | tf_op jit(solution)/shard_map/all_to_all | solution.py:134
  402.1 31.1 %all-to-all-done.2 = bf16[16,2,21504]{2,1,0:T(2,128)(2,1)S(1)} async-done(((bf16[16,2,21504]{2,1,0:T(2,128)(2,1)}), bf16[16,2,21504]{2,1,0:T(2,128)(2,1)S(1)}, u32[]{:S(2)}, u32[]{:S(2)}) %all-to-all-start.2) | async-done | bytes 1376288 | tf_op jit(solution)/shard_map/all_to_all | solution.py:134
  433.2 7.1 %reshape.371 = bf16[7168,1,96]{2,1,0:T(2,128)(2,1)} reshape(bf16[16,2,21504]{2,1,0:T(2,128)(2,1)S(1)} %all-to-all-done.2) | data formatting | bytes 2752512
  440.3 7.7 %bitcast_convert_fusion = f32[1,96,7168]{1,0,2:T(1,128)} fusion(bf16[7168,1,96]{2,1,0:T(2,128)(2,1)} %reshape.371), kind=kLoop, calls=%fused_computation.116 | loop fusion | flops 688128 | bytes 4128768 | tf_op jit(solution)/shard_map/convert_element_type | solution.py:136
  448.1 5.0 %copy.107 = f32[1,96,16,448]{3,1,2,0:T(8,128)} copy(f32[1,96,16,448]{1,3,2,0:T(8,128)} %bitcast.75) | data formatting | bytes 5505024 | tf_op jit(solution)/shard_map/convert_element_type | solution.py:136
  453.1 6.0 %gather_fusion.4 = f32[1024,448]{1,0:T(8,128)S(1)} fusion(f32[1536,448]{1,0:T(8,128)} %bitcast.73, s32[1024]{0:T(1024)S(1)} %broadcast_clamp_fusion), kind=kCustom, calls=%fused_computation.4 | custom fusion | bytes 3674112 | tf_op jit(solution)/shard_map/jit(_take)/gather | solution.py:149
  (92 shorter events, 20.5 us)
Async XLA Ops:
  6.5 6.4 %copy-start = (bf16[12,64,576]{2,1,0:T(8,128)(2,1)S(1)}, bf16[12,64,576]{2,1,0:T(8,128)(2,1)}, u32[]{:S(2)}) copy-start(bf16[12,64,576]{2,1,0:T(8,128)(2,1)} %param.18) | copy-start | bytes 2654212
  18.9 6.7 %copy-start.2 = (s32[192]{0:T(256)S(1)}, s32[192]{0:T(256)}, u32[]{:S(2)}) copy-start(s32[192]{0:T(256)} %param.19) | copy-start | bytes 2308
  18.9 7.6 %copy-start.7 = (bf16[16,64,576]{2,1,0:T(8,128)(2,1)S(1)}, bf16[16,64,576]{2,1,0:T(8,128)(2,1)}, u32[]{:S(2)}) copy-start(bf16[16,64,576]{2,1,0:T(8,128)(2,1)} %param.15) | copy-start | bytes 3538948
  18.9 7.6 %copy-start.8 = (s32[4]{0:T(128)S(1)}, s32[4]{0:T(128)}, u32[]{:S(2)}) copy-start(s32[4]{0:T(128)} %param.17) | copy-start | bytes 52
  18.9 65.4 %all-to-all-start = ((bf16[16,2,64,576]{3,2,1,0:T(8,128)(2,1)}), bf16[16,2,64,576]{3,2,1,0:T(8,128)(2,1)}, u32[]{:S(2)}, u32[]{:S(2)}) async-start(bf16[16,2,64,576]{3,2,1,0:T(8,128)(2,1)} %broadcast_select_fusion.1), calls=%async_computation | async-start | bytes 5242880 | tf_op jit(solution)/shard_map/all_to_all | solution.py:83
  25.5 119.7 %all-gather.2.cloned.1.call-start = ((), (), s32[]{:S(2)}) async-start(), calls=%async_computation.4 | async-start | bytes 4456448 | tf_op jit(solution)/shard_map/all_gather | solution.py:96
  87.4 0.7 copy-start.9
  89.8 6.2 %copy-start.4 = (s32[256,8]{0,1:T(8,128)S(1)}, s32[256,8]{0,1:T(8,128)}, u32[]{:S(2)}) copy-start(s32[256,8]{0,1:T(8,128)} %param.24) | copy-start | bytes 24580
  95.7 82.9 %all-reduce.2.cloned.1.call-start = ((), (), s32[]{:S(2)}) async-start(), calls=%async_computation.5 | async-start | bytes 917504 | tf_op jit(solution)/shard_map/psum | solution.py:115
  99.6 79.1 %copy-start.3 = (bf16[256,448]{0,1:T(8,128)(2,1)S(1)}, bf16[256,448]{0,1:T(8,128)(2,1)}, u32[]{:S(2)}) copy-start(bf16[256,448]{0,1:T(8,128)(2,1)} %param.23) | copy-start | bytes 688132
  196.5 6.7 %copy-start.5 = (bf16[7168]{0:T(1024)(128)(2,1)S(1)}, bf16[7168]{0:T(1024)(128)(2,1)}, u32[]{:S(2)}) copy-start(bf16[7168]{0:T(1024)(128)(2,1)} %param.26) | copy-start | bytes 43012
  196.5 76.6 %all-to-all-start.1 = ((bf16[16,192,448]{2,1,0:T(8,128)(2,1)}), bf16[16,192,448]{2,1,0:T(8,128)(2,1)}, u32[]{:S(2)}, u32[]{:S(2)}) async-start(bf16[16,192,448]{2,1,0:T(8,128)(2,1)} %broadcast_select_fusion), calls=%async_computation.1 | async-start | bytes 6291456 | tf_op jit(solution)/shard_map/all_to_all | solution.py:121
  203.1 139.0 %reduce-scatter.2.cloned.1.call-start = ((), (), s32[]{:S(2)}) async-start(), calls=%async_computation.6 | async-start | bytes 4128768 | tf_op jit(solution)/shard_map/reduce_scatter | solution.py:131
  390.9 11.0 %copy-start.6 = (f32[256,8]{0,1:T(8,128)S(1)}, f32[256,8]{0,1:T(8,128)}, u32[]{:S(2)}) copy-start(f32[256,8]{0,1:T(8,128)} %param.25) | copy-start | bytes 24580
  394.8 38.4 %all-to-all-start.2 = ((bf16[16,2,21504]{2,1,0:T(2,128)(2,1)}), bf16[16,2,21504]{2,1,0:T(2,128)(2,1)S(1)}, u32[]{:S(2)}, u32[]{:S(2)}) async-start(bf16[16,2,21504]{2,1,0:T(2,128)(2,1)} %reshape.370), calls=%async_computation.3 | async-start | bytes 2752512 | tf_op jit(solution)/shard_map/all_to_all | solution.py:134
  453.1 9.2 %copy-start.1 = (bf16[12,64,576]{2,1,0:T(8,128)(2,1)S(1)}, bf16[12,64,576]{2,1,0:T(8,128)(2,1)}, u32[]{:S(2)}) copy-start(bf16[12,64,576]{2,1,0:T(8,128)(2,1)} %param.18) | copy-start | bytes 2654212
Sparse Core Ops, SparseCore 0:
  95.9 49.3 all-gather.1
  152.6 26.0 all-reduce.1
  304.7 37.4 reduce-scatter.1
where the time goes:
time: 470 us; the launch traced here: 469 us
  waiting for transfers between devices  252 us (54%)
  local copies, waits for them, and re-layouts  72.9 us (16%)
  other arithmetic  72.3 us (15%)
  matrix products  38.2 us (8%)
  starting transfers between devices  20.1 us (4%)
  between operations  13.5 us (3%)
    all_to_all x1, waiting for transfers between devices, per_device(): lax.all_to_all(gathered, 'expert', split_axis=0, concat_axis=2, tiled=True)  69.9 us
    all_to_all x1, waiting for transfers between devices, per_device(): lax.all_to_all(outgoing, 'expert', split_axis=0, concat_axis=0, tiled=True)  49.6 us
    all_gather x1, waiting for transfers between devices, per_device(): lax.all_gather(attention, 'expert', axis=0, tiled=True)  45.6 us
    unnamed x1, other arithmetic  39.8 us
    reduce_scatter x1, waiting for transfers between devices, per_device(): lax.psum_scatter(partial_value.astype(jnp.bfloat16), 'head', scatter_dime...  37.6 us
    all_to_all x1, waiting for transfers between devices, per_device(): lax.all_to_all(shared.astype(jnp.bfloat16), 'expert', split_axis=2, conca...  31.1 us
    psum x1, waiting for transfers between devices, per_device(): summed = lax.psum(mixed, 'head')  18 us
    gather x1, local copies, waits for them, and re-layouts, per_device(): jnp.take(hidden_all, slot_rows, axis=0, mode='fill', fill_value=0)  13.2 us
  transfers between devices with their start and end apart: 6, of which 6 were waited for; matrix products, arithmetic and copies ran while one was open for 5% of the time, Pallas kernels for 0%

commit v1 on v0

v1 whole, which is shorter than its diff:
```python
import jax
import jax.numpy as jnp
from jax import lax
from jax.sharding import PartitionSpec as P

ROPE = 64
NOPE = 128


def attend(queries, caches, length, value_up):
    inverse_root = (NOPE + ROPE) ** (-0.5)
    latent_width = value_up.shape[1]
    scores = (
        jnp.einsum("rhc,rtc->rht", queries, caches, preferred_element_type=jnp.float32)
        * inverse_root
    )
    inside = lax.broadcasted_iota(jnp.int32, scores.shape, 2) < length[:, None, None]
    scores = jnp.where(inside, scores, -jnp.inf)
    highest = jnp.max(scores, axis=2, keepdims=True)
    raised = jnp.exp(scores - highest)
    weights = (raised / jnp.sum(raised, axis=2, keepdims=True)).astype(jnp.bfloat16)
    latent = jnp.einsum(
        "rht,rtc->rhc", weights, caches[:, :, :latent_width], preferred_element_type=jnp.float32
    ).astype(jnp.bfloat16)
    values = jnp.einsum(
        "rhc,hcv->rhv", latent, value_up, preferred_element_type=jnp.float32
    ).astype(jnp.bfloat16)
    return values.reshape(values.shape[0], -1)


def earlier_equal(labels):
    count = labels.shape[0]
    position = jnp.arange(count, dtype=jnp.int32)
    before = (labels[:, None] == labels[None, :]) & (position[None, :] < position[:, None])
    return jnp.sum(before.astype(jnp.int32), axis=1)


def per_device(
    queries,
    resident_cache,
    resident_len,
    new_cache,
    new_len,
    new_owner,
    value_up,
    w_output,
    residual,
    expert_ids,
    expert_gates,
    norm_gain,
    w_gate,
    w_up,
    w_down,
):
    n_expert = lax.axis_size("expert")
    n_head = lax.axis_size("head")
    owner_index = lax.axis_index("expert")
    head_index = lax.axis_index("head")
    req_count = resident_cache.shape[0]
    new_count, new_span, cache_width = new_cache.shape
    rows_dev = req_count + new_count
    rows_all = rows_dev * n_expert
    local_experts = w_gate.shape[0]
    most = max(2, (4 * new_count + 3 * n_expert - 1) // (3 * n_expert))
    block_rows = rows_all // n_head
    piece = new_span // n_head

    targets = lax.dynamic_slice_in_dim(new_owner, owner_index * new_count, new_count)
    places = targets * most + earlier_equal(targets)
    slots = jnp.arange(n_expert * most, dtype=jnp.int32)
    senders = jnp.sum(
        jnp.where(
            places[None, :] == slots[:, None], jnp.arange(new_count, dtype=jnp.int32)[None, :], 0
        ),
        axis=1,
    )
    share = lax.dynamic_slice_in_dim(new_cache, head_index * piece, piece, axis=1)
    outgoing = jnp.take(share, senders, axis=0, mode="clip").reshape(
        n_expert, most, piece, cache_width
    )
    incoming = lax.all_to_all(outgoing, "expert", split_axis=0, concat_axis=0, tiled=True)
    position = jnp.arange(new_owner.shape[0], dtype=jnp.int32)
    named = new_owner == owner_index
    before = jnp.sum((named[None, :] & (position[None, :] < position[:, None])).astype(jnp.int32), 1)
    chosen = jnp.sum(
        jnp.where(
            named[None, :]
            & (before[None, :] == jnp.arange(new_count, dtype=jnp.int32)[:, None]),
            position[None, :],
            0,
        ),
        axis=1,
    )
    anchor = chosen // new_count
    arrived_share = jnp.take(
        incoming.reshape(n_expert * most, piece, cache_width),
        anchor * most + earlier_equal(anchor),
        axis=0,
        mode="clip",
    )
    arrived = lax.all_gather(arrived_share, "head", axis=1, tiled=True)
    resident_att = attend(queries[:req_count], resident_cache, resident_len, value_up)
    arrived_att = attend(queries[req_count:], arrived, new_len[chosen], value_up)
    attention = jnp.concatenate([resident_att, arrived_att], axis=0)
    mixed = jnp.dot(
        lax.all_gather(attention, "expert", axis=0, tiled=True),
        w_output,
        preferred_element_type=jnp.float32,
    ).T
    swap = [(0, 1), (1, 0)]
    if n_head == 2:
        mixed = mixed.astype(jnp.bfloat16)
        summed = mixed.astype(jnp.float32) + lax.ppermute(mixed, "head", swap).astype(jnp.float32)
    else:
        summed = lax.psum(mixed, "head")
    hidden = (residual.T.astype(jnp.float32) + summed).astype(jnp.bfloat16)
    hidden_block = lax.dynamic_slice_in_dim(hidden, head_index * block_rows, block_rows, axis=1)

    inputs = lax.all_gather(hidden, "expert", axis=0, tiled=True).astype(jnp.float32)
    inverse = lax.rsqrt(jnp.mean(inputs * inputs, axis=0, keepdims=True) + 1e-06)
    normed = (inputs * inverse * norm_gain.astype(jnp.float32)[:, None]).astype(jnp.bfloat16)
    partial = None
    for e in range(local_experts):
        gate_act = jnp.einsum("df,dr->fr", w_gate[e], normed, preferred_element_type=jnp.float32)
        up_act = jnp.einsum("df,dr->fr", w_up[e], normed, preferred_element_type=jnp.float32)
        act = (jax.nn.silu(gate_act) * up_act).astype(jnp.bfloat16)
        down = jnp.einsum("fd,fr->dr", w_down[e], act, preferred_element_type=jnp.float32)
        mine = expert_ids == owner_index * local_experts + e
        weight = jnp.sum(jnp.where(mine, expert_gates, 0.0), axis=1)
        term = down * weight[None, :]
        partial = term if partial is None else partial + term
    routed = lax.psum_scatter(
        partial.astype(jnp.bfloat16), "expert", scatter_dimension=0, tiled=True
    )
    if n_head == 2:
        kept = lax.dynamic_slice_in_dim(routed, head_index * block_rows, block_rows, axis=1)
        sent = lax.dynamic_slice_in_dim(routed, (1 - head_index) * block_rows, block_rows, axis=1)
        got = lax.ppermute(sent, "head", swap)
        routed_block = kept.astype(jnp.float32) + got.astype(jnp.float32)
    else:
        routed_block = lax.psum_scatter(
            routed, "head", scatter_dimension=1, tiled=True
        ).astype(jnp.float32)
    return (hidden_block.astype(jnp.float32) + routed_block).astype(jnp.bfloat16).T


def solution(mesh):
    return jax.shard_map(
        per_device,
        mesh=mesh,
        in_specs=(
            P("expert", "head", None),
            P("expert", None, None),
            P("expert"),
            P("expert", None, None),
            P(),
            P(),
            P("head", None, None),
            P("head", "expert"),
            P(None, "expert"),
            P(),
            P(),
            P(),
            P("expert", None, "head"),
            P("expert", None, "head"),
            P("expert", "head", None),
        ),
        out_specs=P("head", "expert"),
        check_vma=False,
    )
```

time: 470 us -> 291 us (0.62)
  local copies, waits for them, and re-layouts: 72.9 us -> 5.83 us
  other arithmetic: 72.3 us -> 8.7 us
  waiting for transfers between devices: 252 us -> 191 us
  blocking collectives: 0 us -> 13.3 us
  starting transfers between devices: 20.1 us -> 9.3 us
  matrix products: 38.2 us -> 44.4 us
    all_to_all x2 -> x0, waiting for transfers between devices: 101 us -> none  [the longest x1 69.9 us: per_device(): lax.all_to_all(gathered, 'expert', split_axis=0, concat_axis=2, tiled=True)]
    all_gather x0 -> x1, waiting for transfers between devices: none -> 47.1 us  [per_device(): lax.all_gather(hidden, 'expert', axis=0, tiled=True).astype(jnp.float32)]
    unnamed x1 -> x0, other arithmetic: 39.8 us -> none
    all_to_all x1, waiting for transfers between devices: 49.6 us -> 19.8 us  [per_device(): lax.all_to_all(outgoing, 'expert', split_axis=0, concat_axis=0, tiled=True)]
    reduce_scatter x1, waiting for transfers between devices: 37.6 us -> 65.8 us  [per_device(): lax.psum_scatter(partial.astype(jnp.bfloat16), 'expert', scatter_dimensio...]
    gather x4 -> x2, local copies, waits for them, and re-layouts: 24.1 us -> 2.39 us  [the longest x1 1.76 us: per_device(): jnp.take(share, senders, axis=0, mode='clip')]
    psum x1 -> x0, waiting for transfers between devices: 18 us -> none  [per_device(): summed = lax.psum(mixed, 'head')]
    convert_element_type x4 -> x0, local copies, waits for them, and re-layouts: 15 us -> none  [the longest x2 9.82 us: per_device(): (inputs * inverse * norm_gain.astype(jnp.float32)).astype(jnp.bfloat16)]
  transfers between devices with their start and end apart: 6 -> 6, of which waited for: 6 -> 6; matrix products, arithmetic and copies ran while one was open for 5% -> 4% of each run, Pallas kernels for 0% -> 0%
where the time goes in v1:
time: 291 us; the launch traced here: 286 us
  waiting for transfers between devices  191 us (66%)
  matrix products  44.4 us (15%)
  blocking collectives  13.3 us (5%)
  between operations  13.3 us (5%)
  starting transfers between devices  9.3 us (3%)
  other arithmetic  8.7 us (3%)
  local copies, waits for them, and re-layouts  5.83 us (2%)
    reduce_scatter x1, waiting for transfers between devices, per_device(): lax.psum_scatter(partial.astype(jnp.bfloat16), 'expert', scatter_dimensio...  65.8 us
    all_gather x1, waiting for transfers between devices, per_device(): lax.all_gather(attention, 'expert', axis=0, tiled=True)  50.2 us
    all_gather x1, waiting for transfers between devices, per_device(): lax.all_gather(hidden, 'expert', axis=0, tiled=True).astype(jnp.float32)  47.1 us
    all_to_all x1, waiting for transfers between devices, per_device(): lax.all_to_all(outgoing, 'expert', split_axis=0, concat_axis=0, tiled=True)  19.8 us
    all_gather x1, blocking collectives, per_device(): arrived = lax.all_gather(arrived_share, 'head', axis=1, tiled=True)  13.3 us
    dot_general x1, matrix products, per_device(): jnp.einsum('fd,fr->dr', w_down[e], act, preferred_element_type=jnp.float32)  13.2 us
    dot_general x2, matrix products, attend(): jnp.einsum('rhc,hcv->rhv', latent, value_up, preferred_element_type=jnp.f...  9.42 us
    dot_general x1, matrix products, per_device(): jnp.einsum('df,dr->fr', w_gate[e], normed, preferred_element_type=jnp.flo...  8.31 us
  transfers between devices with their start and end apart: 6, of which 6 were waited for; matrix products, arithmetic and copies ran while one was open for 4% of the time, Pallas kernels for 0%

profile of v1, /device:TPU:13, one launch (start us, length us, event | category | flops | bytes accessed | tf_op | source)
XLA Modules:
  0.0 285.9 jit_solution(2620647868807348800)
XLA Ops:
  6.5 0.8 dynamic_slice.16
  7.6 0.8 multiply_add_fusion
  8.5 1.8 gather_fusion.1
  10.2 6.5 %all-to-all-start = ((bf16[16,2,32,576]{3,2,1,0:T(8,128)(2,1)}), bf16[16,2,32,576]{3,2,1,0:T(8,128)(2,1)S(1)}, u32[]{:S(2)}, u32[]{:S(2)}) async-start(bf16[16,2,32,576]{3,2,1,0:T(8,128)(2,1)} %bitcast.5), calls=%async_computation | async-start | bytes 2621440 | tf_op jit(solution)/shard_map/all_to_all | solution.py:81
  16.8 0.7 broadcast_compare_fusion
  18.0 1.3 gather_fusion
  19.3 1.7 fusion.33
  21.0 0.2 fusion.65
  21.2 1.8 convolution_convert_fusion.2
  23.0 4.6 %fusion.35 = bf16[4,8192]{1,0:T(4,128)(2,1)S(1)} fusion(bf16[64,512,128]{2,1,0:T(8,128)(2,1)} %param.21, bf16[4,64,512]{2,1,0:T(8,128)(2,1)S(1)} %convolution_convert_fusion.2), kind=kOutput, calls=%fused_computation.38 | convolution fusion | flops 33587200 | bytes 8716288 | tf_op jit(solution)/shard_map/rhc,hcv->rhv/dot_general | solution.py:25
  27.6 19.8 %all-to-all-done = bf16[16,2,32,576]{3,2,1,0:T(8,128)(2,1)S(1)} async-done(((bf16[16,2,32,576]{3,2,1,0:T(8,128)(2,1)}), bf16[16,2,32,576]{3,2,1,0:T(8,128)(2,1)S(1)}, u32[]{:S(2)}, u32[]{:S(2)}) %all-to-all-start) | async-done | bytes 1179680 | tf_op jit(solution)/shard_map/all_to_all | solution.py:81
  47.3 0.6 gather_fusion.2
  48.0 13.3 %all-gather = bf16[12,64,576]{2,1,0:T(8,128)(2,1)S(1)} all-gather(bf16[12,32,576]{2,1,0:T(8,128)(2,1)S(1)} %gather_fusion.2), channel_id=2, replica_groups=mesh['head'=2,'expert'=16] {'head'}, dimensions={1}, use_global_device_ids=true | all-gather | bytes 1327104 | tf_op jit(solution)/shard_map/all_gather | solution.py:101
  61.3 2.0 fusion.25
  63.5 1.6 convolution_convert_fusion
  65.0 4.8 %fusion.32 = bf16[12,64,128]{2,0,1:T(8,128)(2,1)S(1)} fusion(bf16[64,512,128]{2,1,0:T(8,128)(2,1)} %param.21, bf16[12,64,512]{2,1,0:T(8,128)(2,1)S(1)} %convolution_convert_fusion), kind=kOutput, calls=%fused_computation.33 | convolution fusion | flops 100761600 | bytes 9371648 | tf_op jit(solution)/shard_map/rhc,hcv->rhv/dot_general | solution.py:25
  70.1 0.8 pad_maximum_fusion
  71.0 50.2 %all-gather.4.cloned.1.call-done = bf16[256,8192]{1,0:T(8,128)(2,1)} async-done(((bf16[16,8192]{1,0:T(8,128)(2,1)}), bf16[256,8192]{1,0:T(8,128)(2,1)}) %all-gather.4.cloned.1.call-update) | async-done | bytes 4194320 | tf_op jit(solution)/shard_map/all_gather | solution.py:106
  121.2 6.4 %fusion.34 = bf16[448,256]{1,0:T(8,128)(2,1)S(1)} fusion(bf16[256,8192]{1,0:T(8,128)(2,1)} %all-gather.4.cloned.1.call-done, bf16[8192,448]{0,1:T(8,128)(2,1)} %param.22), kind=kOutput, calls=%fused_computation.36 | convolution fusion | flops 1879162880 | bytes 11763712 | tf_op jit(solution)/shard_map/dot_general | solution.py:105
  127.7 1.3 collective-permute-start
  128.9 5.7 %collective-permute-done = bf16[448,256]{1,0:T(8,128)(2,1)S(1)} collective-permute-done((bf16[448,256]{1,0:T(8,128)(2,1)S(1)}, bf16[448,256]{1,0:T(8,128)(2,1)S(1)}, u32[]{:S(2)}, u32[]{:S(2)}) %collective-permute-start) | collective-permute-done | bytes 229408 | tf_op jit(solution)/shard_map/ppermute | solution.py:113
  134.6 0.8 fusion.48
  135.4 0.2 reduce-scatter.2.cloned.1.call-start
  135.7 47.1 %all-gather.6.cloned.1.call-done = bf16[7168,256]{1,0:T(8,128)(2,1)} async-done(((bf16[448,256]{1,0:T(8,128)(2,1)}), bf16[7168,256]{1,0:T(8,128)(2,1)}) %all-gather.6.cloned.1.call-update) | async-done | bytes 3670032 | tf_op jit(solution)/shard_map/all_gather | solution.py:119
  182.8 3.0 %fusion.4 = f32[256]{0:T(256)S(1)} fusion(bf16[7168,256]{1,0:T(8,128)(2,1)} %all-gather.6.cloned.1.call-done), kind=kLoop, calls=%fused_computation.10 | loop fusion | flops 5504768 | bytes 3671040 | tf_op jit(solution)/shard_map/reduce_sum | solution.py:120
  185.9 8.3 %fusion.13 = f32[512,256]{0,1:T(8,128)S(1)} fusion(bf16[1,7168,512]{2,1,0:T(8,128)(2,1)} %param.27, bf16[7168,256]{1,0:T(8,128)(2,1)} %all-gather.6.cloned.1.call-done, f32[7168]{0:T(1024)S(1)} %convert_element_type.104, f32[256]{0:T(256)S(1)} %add_rsqrt_fusion), kind=kOutput, calls=%fused_computation.20 | convolution fusion | flops 1886388224 | bytes 11564032 | tf_op jit(solution)/shard_map/df,dr->fr/dot_general | solution.py:124
  194.2 13.2 %fusion.3 = bf16[7168,256]{1,0:T(8,128)(2,1)} fusion(bf16[1,512,7168]{2,1,0:T(8,128)(2,1)} %param.29, f32[256]{0:T(256)S(1)} %select_reduce_fusion.1, bf16[1,7168,512]{2,1,0:T(8,128)(2,1)} %param.28, bf16[7168,256]{1,0:T(8,128)(2,1)} %all-gather.6.cloned.1.call-done, f32[7168]{0:T(1024)S(1)} %convert_element_type.104, f32[256]{0:T(256)S(1)} %add_rsqrt_fusion, ...), kind=kOutput, calls=%fused_computation.9 | convolution fusion | flops 3769892864 | bytes 22575104 | tf_op jit(solution)/shard_map/fd,fr->dr/dot_general | solution.py:127
  207.4 65.8 %reduce-scatter.2.cloned.1.call-done = bf16[448,256]{1,0:T(8,128)(2,1)} async-done(((bf16[7168,256]{1,0:T(8,128)(2,1)}), bf16[448,256]{1,0:T(8,128)(2,1)}) %reduce-scatter.2.cloned.1.call-update) | async-done | bytes 229392 | tf_op jit(solution)/shard_map/reduce_scatter | solution.py:132
  273.2 0.9 constant_dynamic-slice_fusion
  274.1 1.2 collective-permute-start.1
  275.4 2.4 collective-permute-done.1
  277.8 1.6 fusion.54
  (37 shorter events, 1.4 us)
Async XLA Ops:
  6.5 1.9 copy-start
  10.2 37.1 %all-to-all-start = ((bf16[16,2,32,576]{3,2,1,0:T(8,128)(2,1)}), bf16[16,2,32,576]{3,2,1,0:T(8,128)(2,1)S(1)}, u32[]{:S(2)}, u32[]{:S(2)}) async-start(bf16[16,2,32,576]{3,2,1,0:T(8,128)(2,1)} %bitcast.5), calls=%async_computation | async-start | bytes 2621440 | tf_op jit(solution)/shard_map/all_to_all | solution.py:81
  16.8 104.4 %all-gather.4.cloned.1.call-start = ((), (), s32[]{:S(2)}) async-start(), calls=%async_computation.2 | async-start | bytes 4456448 | tf_op jit(solution)/shard_map/all_gather | solution.py:106
  61.3 2.0 copy-start.2
  70.9 63.7 %copy-start.3 = (bf16[256,448]{0,1:T(8,128)(2,1)S(1)}, bf16[256,448]{0,1:T(8,128)(2,1)}, u32[]{:S(2)}) copy-start(bf16[256,448]{0,1:T(8,128)(2,1)} %param.23) | copy-start | bytes 688132
  71.0 64.7 %copy-start.4 = (bf16[7168]{0:T(1024)(128)(2,1)S(1)}, bf16[7168]{0:T(1024)(128)(2,1)}, u32[]{:S(2)}) copy-start(bf16[7168]{0:T(1024)(128)(2,1)} %param.26) | copy-start | bytes 43012
  71.0 64.7 %copy-start.5 = (f32[256,8]{0,1:T(8,128)S(1)}, f32[256,8]{0,1:T(8,128)}, u32[]{:S(2)}) copy-start(f32[256,8]{0,1:T(8,128)} %param.25) | copy-start | bytes 24580
  71.0 64.7 %copy-start.6 = (s32[256,8]{0,1:T(8,128)S(1)}, s32[256,8]{0,1:T(8,128)}, u32[]{:S(2)}) copy-start(s32[256,8]{0,1:T(8,128)} %param.24) | copy-start | bytes 24580
  71.0 111.8 %all-gather.6.cloned.1.call-start = ((), (), s32[]{:S(2)}) async-start(), calls=%async_computation.3 | async-start | bytes 3899392 | tf_op jit(solution)/shard_map/all_gather | solution.py:119
  127.7 7.0 %collective-permute-start = (bf16[448,256]{1,0:T(8,128)(2,1)S(1)}, bf16[448,256]{1,0:T(8,128)(2,1)S(1)}, u32[]{:S(2)}, u32[]{:S(2)}) collective-permute-start(bf16[448,256]{1,0:T(8,128)(2,1)S(1)} %fusion.34), channel_id=1, source_target_pairs={{0,16},{16,0},{1,17},{17,1},{2,18},{18,2},{3,19},{19,3},{4,20},{20... | collective-permute-start | bytes 688136 | tf_op jit(solution)/shard_map/ppermute | solution.py:113
  135.4 137.8 %reduce-scatter.2.cloned.1.call-start = ((), (), s32[]{:S(2)}) async-start(), calls=%async_computation.4 | async-start | bytes 3899392 | tf_op jit(solution)/shard_map/reduce_scatter | solution.py:132
  194.2 83.6 %copy-start.1 = (bf16[448,256]{1,0:T(8,128)(2,1)S(1)}, bf16[448,256]{1,0:T(8,128)(2,1)}, u32[]{:S(2)}) copy-start(bf16[448,256]{1,0:T(8,128)(2,1)} %fusion.48) | copy-start | bytes 688132
  274.1 3.6 %collective-permute-start.1 = (bf16[448,128]{1,0:T(8,128)(2,1)S(1)}, bf16[448,128]{1,0:T(8,128)(2,1)S(1)}, u32[]{:S(2)}, u32[]{:S(2)}) collective-permute-start(bf16[448,128]{1,0:T(8,128)(2,1)S(1)} %constant_dynamic-slice_fusion), channel_id=1, source_target_pairs={{0,16},{16,0},{1,17},{17,1},{2,18},{18,2},{3,19},{19,3},{4,20},{20... | collective-permute-start | bytes 344072 | tf_op jit(solution)/shard_map/ppermute | solution.py:138
Sparse Core Ops, SparseCore 0:
  71.1 50.0 all-gather.3
  135.5 47.2 all-gather.5
  207.5 65.6 reduce-scatter.1
